TPU v7x, 32 devices: a whole 2x2x4 slice. The times are simulated.
32 devices in a mesh: grp: 4 (over x, core), tbl: 8 (over z, y).
Axes of the slice: x: 2, y: 2, z: 4, core: 2. Of those that a mesh axis runs over, the one named last changes fastest.
Arguments:
- cross_input: bfloat16 [4096, 3456], P(('grp', 'tbl')), may hold values from -6 to 6
- upstream: bfloat16 [4096, 3456], P(('grp', 'tbl')), may hold values from -6 to 6
- v_weight: bfloat16 [256, 3456], replicated, may hold values from -0.109375 to 0.109375
- u_weight: bfloat16 [256, 3456], replicated, may hold values from -0.375 to 0.375
- bias: float32 [3456], replicated, may hold values from -3 to 3
- placement: int32 [26], replicated, may hold values from 0 to 7, as said below
- owned_ids: int32 [40, 4, 4096], P('tbl', None, 'grp'), may hold values from 0 to 255
Outputs:
- cross_grad: float32 [256, 6912], P(('grp', 'tbl'))
- table_grad: float32 [40, 256, 128], P('tbl', 'grp')
Inputs may be any that keep to these rules, and one draw needn't show every extreme that they name: `placement`: no device holds more than 5 tables, and some device holds exactly 5.
All inputs are finite; a program needn't handle non-finite values.
Results may differ from a plain program's by a relative error of at most 0.004.
Values may be sent and summed in bfloat16 or wider, within the bound.
A program may use at most 64 MiB of HBM per device.

v0:
```python
import math

import jax
import jax.numpy as jnp
from jax import lax
from jax.sharding import PartitionSpec as P

EMB = 128
TABLES = 26
ROWS = 256


def outer_sum(left, right):
    return jnp.einsum("br,bd->rd", left, right, preferred_element_type=jnp.float32)


def on_device(cross_input, upstream, v_weight, u_weight, bias, placement, owned_ids):
    n_grp = lax.axis_size("grp")
    n_tbl = lax.axis_size("tbl")
    samples = cross_input.shape[0]
    slots_dev = owned_ids.shape[0]
    scale = 1.0 / math.sqrt(samples * n_grp * n_tbl)
    hidden = jnp.dot(cross_input, v_weight.T, preferred_element_type=jnp.float32).astype(
        jnp.bfloat16
    )
    mixed = jnp.dot(hidden, u_weight, preferred_element_type=jnp.float32) + bias
    up_float = upstream.astype(jnp.float32)
    product_grad = (up_float * cross_input.astype(jnp.float32)).astype(jnp.bfloat16)
    hidden_grad = jnp.dot(product_grad, u_weight.T, preferred_element_type=jnp.float32).astype(
        jnp.bfloat16
    )
    input_grad = up_float * (1.0 + mixed) + jnp.dot(
        hidden_grad, v_weight, preferred_element_type=jnp.float32
    )
    pooled = input_grad[:, EMB:].astype(jnp.bfloat16).reshape(samples, TABLES, EMB)
    same = placement[:, None] == placement[None, :]
    earlier = jnp.arange(TABLES)[None, :] < jnp.arange(TABLES)[:, None]
    slot = jnp.sum((same & earlier).astype(jnp.int32), axis=1)
    target = slot * n_tbl + placement
    select = (jnp.arange(slots_dev * n_tbl, dtype=jnp.int32)[:, None] == target[None, :]).astype(
        jnp.bfloat16
    )
    outgoing = jnp.einsum("st,bte->sbe", select, pooled, preferred_element_type=jnp.float32)
    outgoing = outgoing.astype(jnp.bfloat16).reshape(slots_dev, n_tbl, samples, EMB)
    arriving = lax.all_to_all(outgoing, "tbl", split_axis=1, concat_axis=1, tiled=True)
    arriving = arriving.reshape(slots_dev, n_tbl * samples, EMB)
    row_numbers = jnp.arange(ROWS, dtype=jnp.int32)
    counts = jnp.sum(
        (owned_ids[:, :, None, :] == row_numbers[None, None, :, None]).astype(jnp.bfloat16), axis=1
    )
    row_terms = jnp.einsum("srm,sme->sre", counts, arriving, preferred_element_type=jnp.float32)
    table_grad = lax.psum_scatter(row_terms, "grp", scatter_dimension=1, tiled=True)
    term = jnp.concatenate(
        [outer_sum(hidden, product_grad), outer_sum(hidden_grad, cross_input)], axis=1
    )
    summed = lax.psum_scatter(term, ("grp", "tbl"), scatter_dimension=0, tiled=True)
    cross_grad = summed * scale
    return (cross_grad, table_grad)


def solution(mesh):
    in_specs = (
        P(("grp", "tbl"), None),
        P(("grp", "tbl"), None),
        P(),
        P(),
        P(),
        P(),
        P("tbl", None, "grp"),
    )
    out_specs = (P(("grp", "tbl"), None), P("tbl", "grp", None))
    return jax.shard_map(
        on_device, mesh=mesh, in_specs=in_specs, out_specs=out_specs, check_vma=False
    )
```

profile of v0, /device:TPU:0, one launch (start us, length us, event | category | flops | bytes accessed | tf_op | source)
XLA Modules:
  0.0 169.9 jit_solution(12001875181605455586)
XLA Ops:
  7.2 0.0 copy-start
  7.2 0.0 reduce-scatter.3.cloned.1.call-start
  7.2 2.9 %convolution_convert_fusion.1 = bf16[128,256]{1,0:T(8,128)(2,1)S(1)} fusion(bf16[256,3456]{1,0:T(8,128)(2,1)} %param.10, bf16[128,3456]{1,0:T(8,128)(2,1)} %param.7, bf16[128,3456]{1,0:T(8,128)(2,1)} %param.8), kind=kOutput, calls=%fused_computation.12 | convolution fusion | flops 228294656 | bytes 3604480 | tf_op jit(solution)/shard_map/dot_general | solution.py:29
  10.2 0.7 fusion.10
  10.8 0.7 convolution_convert_fusion.2
  11.6 0.5 copy-done.3
  12.0 0.7 fusion.5
  12.7 3.4 %pad_maximum_fusion = f32[256,6912]{1,0:T(8,128)} fusion(f32[256,3456]{1,0:T(8,128)S(1)} %fusion.10, f32[256,3456]{1,0:T(8,128)S(1)} %fusion.5), kind=kLoop, calls=%fused_computation.3 | loop fusion | flops 1769472 | bytes 14155776 | tf_op jit(solution)/shard_map/concatenate | solution.py:53
  16.1 0.0 reduce-scatter.3.cloned.1.call-update
  16.1 0.1 convert_element_type.29
  16.2 0.6 copy-done.10
  16.8 0.1 copy-done.6
  17.0 0.4 fusion.12
  17.4 1.1 copy-done.4
  18.4 0.4 fusion.11
  18.9 0.3 fusion.2
  19.1 1.3 copy.21
  20.4 1.9 %copy.22 = bf16[128,26,128]{2,1,0:T(8,128)(2,1)S(1)} copy(bf16[128,26,128]{0,2,1:T(8,128)(2,1)} %bitcast.21) | data formatting | bytes 1703936 | tf_op jit(solution)/shard_map/reshape | solution.py:35
  22.3 0.2 convert_reduce_fusion
  22.5 0.6 fusion.4
  23.2 1.4 copy.23
  24.6 7.4 %all-to-all-start = ((bf16[5,8,128,128]{3,2,0,1:T(8,128)(2,1)}), bf16[5,8,128,128]{3,2,0,1:T(8,128)(2,1)S(1)}, u32[]{:S(2)}, u32[]{:S(2)}) async-start(bf16[5,8,128,128]{3,2,0,1:T(8,128)(2,1)} %copy.23), calls=%async_computation.1 | async-start | bytes 2621440 | tf_op jit(solution)/shard_map/all_to_all | solution.py:45
  32.0 0.0 reduce-scatter.5.cloned.1.call-start
  32.1 4.8 %fusion.1 = bf16[5,256,1024]{2,1,0:T(8,128)(2,1)} fusion(s32[5,4,1024]{2,1,0:T(4,128)S(1)} %copy-done.9), kind=kLoop, calls=%fused_computation.2 | loop fusion | flops 14417920 | bytes 2703360 | tf_op jit(solution)/shard_map/reduce_sum | solution.py:48
  36.9 26.5 %all-to-all-done = bf16[5,8,128,128]{3,2,0,1:T(8,128)(2,1)S(1)} async-done(((bf16[5,8,128,128]{3,2,0,1:T(8,128)(2,1)}), bf16[5,8,128,128]{3,2,0,1:T(8,128)(2,1)S(1)}, u32[]{:S(2)}, u32[]{:S(2)}) %all-to-all-start) | async-done | bytes 1310752 | tf_op jit(solution)/shard_map/all_to_all | solution.py:45
  63.4 0.1 copy.24
  63.5 1.6 copy-done.2
  65.1 1.7 fusion.13
  66.8 0.0 reduce-scatter.5.cloned.1.call-update
  66.8 71.8 %reduce-scatter.3.cloned.1.call-done = f32[8,6912]{1,0:T(8,128)} async-done(((f32[256,6912]{1,0:T(8,128)}), f32[8,6912]{1,0:T(8,128)}) %reduce-scatter.3.cloned.1.call-update) | async-done | bytes 221200 | tf_op jit(solution)/shard_map/reduce_scatter | solution.py:56
  138.6 1.6 broadcast_multiply_fusion
  140.2 22.8 %reduce-scatter.5.cloned.1.call-done = f32[5,64,128]{2,1,0:T(8,128)} async-done(((f32[5,256,128]{2,1,0:T(8,128)}), f32[5,64,128]{2,1,0:T(8,128)}) %reduce-scatter.5.cloned.1.call-update) | async-done | bytes 163856 | tf_op jit(solution)/shard_map/reduce_scatter | solution.py:52
  (20 shorter events, 0.1 us)
Async XLA Ops:
  7.2 3.7 %copy-start = (bf16[256,3456]{1,0:T(8,128)(2,1)S(1)}, bf16[256,3456]{1,0:T(8,128)(2,1)}, u32[]{:S(2)}) copy-start(bf16[256,3456]{1,0:T(8,128)(2,1)} %param.9) | copy-start | bytes 5308420
  7.2 3.0 %copy-start.1 = (bf16[128,3456]{1,0:T(8,128)(2,1)S(1)}, bf16[128,3456]{1,0:T(8,128)(2,1)}, u32[]{:S(2)}) copy-start(bf16[128,3456]{1,0:T(8,128)(2,1)} %param.7) | copy-start | bytes 2654212
  7.2 131.4 %reduce-scatter.3.cloned.1.call-start = ((), (), s32[]{:S(2)}) async-start(), calls=%async_computation.3 | async-start | bytes 7299072 | tf_op jit(solution)/shard_map/reduce_scatter | solution.py:56
  10.1 0.7 copy-start.5
  10.8 1.2 copy-start.3
  12.0 0.7 copy-start.7
  16.1 0.7 copy-start.10
  16.1 0.8 copy-start.6
  17.0 1.5 copy-start.4
  17.0 1.5 copy-start.8
  19.1 3.2 %copy-start.11 = (s32[26]{0:T(128)S(1)}, s32[26]{0:T(128)}, u32[]{:S(2)}) copy-start(s32[26]{0:T(128)} %param.12) | copy-start | bytes 316
  24.6 7.5 %copy-start.9 = (s32[5,4,1024]{2,1,0:T(4,128)S(1)}, s32[5,4,1024]{2,1,0:T(4,128)}, u32[]{:S(2)}) copy-start(s32[5,4,1024]{2,1,0:T(4,128)} %param.13) | copy-start | bytes 245764
  24.6 38.8 %all-to-all-start = ((bf16[5,8,128,128]{3,2,0,1:T(8,128)(2,1)}), bf16[5,8,128,128]{3,2,0,1:T(8,128)(2,1)S(1)}, u32[]{:S(2)}, u32[]{:S(2)}) async-start(bf16[5,8,128,128]{3,2,0,1:T(8,128)(2,1)} %copy.23), calls=%async_computation.1 | async-start | bytes 2621440 | tf_op jit(solution)/shard_map/all_to_all | solution.py:45
  32.0 131.1 %reduce-scatter.5.cloned.1.call-start = ((), (), s32[]{:S(2)}) async-start(), calls=%async_computation.4 | async-start | bytes 819200 | tf_op jit(solution)/shard_map/reduce_scatter | solution.py:52
  63.4 1.7 %copy-start.2 = (bf16[5,256,1024]{2,1,0:T(8,128)(2,1)S(1)}, bf16[5,256,1024]{2,1,0:T(8,128)(2,1)}, u32[]{:S(2)}) copy-start(bf16[5,256,1024]{2,1,0:T(8,128)(2,1)} %fusion.1) | copy-start | bytes 7864324
Sparse Core Ops, SparseCore 0:
  16.2 122.3 reduce-scatter.2
  141.7 21.3 reduce-scatter.4
where the time goes:
time: 170 us
  waiting for transfers between devices  121 us (71%)
  between operations  14.2 us (8%)
  other arithmetic  10.4 us (6%)
  local copies, waits for them, and re-layouts  8.59 us (5%)
  matrix products  8.03 us (5%)
  starting transfers between devices  7.52 us (4%)
    reduce_scatter x1, waiting for transfers between devices, on_device(): lax.psum_scatter(term, ('grp', 'tbl'), scatter_dimension=0, tiled=True)  71.8 us
    all_to_all x1, waiting for transfers between devices, on_device(): lax.all_to_all(outgoing, 'tbl', split_axis=1, concat_axis=1, tiled=True)  26.5 us
    reduce_scatter x1, waiting for transfers between devices, on_device(): lax.psum_scatter(row_terms, 'grp', scatter_dimension=1, tiled=True)  22.8 us
    all_to_all x1, starting transfers between devices, on_device(): lax.all_to_all(outgoing, 'tbl', split_axis=1, concat_axis=1, tiled=True)  7.44 us
    reduce_sum x1, other arithmetic, on_device(): jnp.sum((owned_ids[:, :, None, :] == row_numbers[None, None, :, None]).as...  4.81 us
    unnamed x24, local copies, waits for them, and re-layouts  3.86 us
  transfers between devices with their start and end apart: 3, of which 3 were waited for; matrix products, arithmetic and copies ran while one was open for 9% of the time, Pallas kernels for 0%

commit v1 on v0

--- a/solution.py
+++ b/solution.py
@@ -1,13 +1,17 @@
+import functools
 import math
 
 import jax
 import jax.numpy as jnp
 from jax import lax
+from jax.experimental import pallas as pl
+from jax.experimental.pallas import tpu as pltpu
 from jax.sharding import PartitionSpec as P
 
 EMB = 128
 TABLES = 26
 ROWS = 256
+MESH = pl.DeviceIdType.MESH
 
 
 def outer_sum(left, right):
@@ -56,6 +60,291 @@
     summed = lax.psum_scatter(term, ("grp", "tbl"), scatter_dimension=0, tiled=True)
     cross_grad = summed * scale
     return (cross_grad, table_grad)
+
+
+def flip_stages(n_grp, n_tbl):
+    return n_grp == 4 and n_tbl == 8
+
+
+def fused_body(
+    n_grp, n_tbl, scale, cut,
+    ci_ref, up_ref, v_ref, u_ref, bias_ref, place_ref, inv_ref, ids_ref,
+    cross_ref, table_ref,
+    ci2, up2, pg, hid, hgr, hid_t, hgr_t, ids_in,
+    sa, sb, st, ra1, ra2, ra3, ra4, rb1, rb2, rb3, rb4, rt1, rt2, rt3, rt4,
+    pa1, pa2, pa3, pb1, pb2, pb3, pt1, pte, pt2, pt3,
+    ssem, rsem, in_ssem, in_rsem, id_ssem, id_rsem,
+):
+    f32, bf16 = jnp.float32, jnp.bfloat16
+    g = lax.axis_index("grp")
+    t = lax.axis_index("tbl")
+    core, x = g % 2, g // 2
+    y, zl, zh = t % 2, (t // 2) % 2, t // 4
+    og = g + 1 - 2 * core
+    xg = core + 2 * (1 - x)
+    yt = t + 1 - 2 * y
+    zlt = t + 2 * (1 - 2 * zl)
+    zht = t + 4 * (1 - 2 * zh)
+    samples, width = ci_ref.shape
+    rank = v_ref.shape[0]
+    slots_dev = ids_ref.shape[0]
+    part = ROWS // n_grp
+
+    barrier = pltpu.get_barrier_semaphore()
+
+    def greet(gg, tt):
+        pl.semaphore_signal(barrier, inc=1, device_id=(gg, tt), device_id_type=MESH)
+
+    for step in range(1, n_tbl):
+        greet(g, (t + step) % n_tbl)
+        greet(og, (t + step) % n_tbl)
+    greet(og, t)
+    greet(xg, t)
+    pl.semaphore_wait(barrier, 2 * n_tbl)
+
+    def send(src, dst, s, r, gg, tt):
+        copy = pltpu.make_async_remote_copy(
+            src_ref=src, dst_ref=dst, send_sem=s, recv_sem=r,
+            device_id=(gg, tt), device_id_type=MESH,
+        )
+        copy.start()
+        return copy
+
+    in_copies = [
+        send(ci_ref, ci2, in_ssem.at[0], in_rsem.at[0], og, t),
+        send(up_ref, up2, in_ssem.at[1], in_rsem.at[1], og, t),
+    ]
+    id_copies = []
+    for step in range(n_tbl):
+        to = (t + step) % n_tbl
+        block = ids_ref.at[:, :, pl.ds(pl.multiple_of(to * samples, samples), samples)]
+        if step == 0:
+            mine = pltpu.make_async_copy(block, ids_in.at[0, t], id_ssem.at[0, 0])
+            mine.start()
+        else:
+            id_copies.append(
+                send(block, ids_in.at[0, t], id_ssem.at[0, step], id_rsem.at[0, step], g, to)
+            )
+        id_copies.append(
+            send(block, ids_in.at[1, t], id_ssem.at[1, step], id_rsem.at[1, step], og, to)
+        )
+
+    nt = (((1,), (1,)), ((), ()))
+
+    def forward(c_in, u_in, row):
+        rows = pl.ds(row, samples)
+        hidden = lax.dot_general(c_in[...], v_ref[...], nt, preferred_element_type=f32)
+        hid[rows, :] = hidden.astype(bf16)
+        hid_t[:, rows] = hidden.T.astype(bf16)
+        pg[rows, :] = (u_in[...].astype(f32) * c_in[...].astype(f32)).astype(bf16)
+        hgrad = lax.dot_general(pg[rows, :], u_ref[...], nt, preferred_element_type=f32)
+        hgr[rows, :] = hgrad.astype(bf16)
+        hgr_t[:, rows] = hgrad.T.astype(bf16)
+
+    forward(ci_ref, up_ref, 0)
+    for copy in in_copies:
+        copy.wait()
+    forward(ci2, up2, samples)
+
+    quarter = rank // n_grp
+
+    def picked(ref):
+        low = ref[pl.ds(pl.multiple_of(core * quarter, quarter), quarter), :]
+        high = ref[pl.ds(pl.multiple_of((core + 2) * quarter, quarter), quarter), :]
+        return jnp.concatenate([low, high], axis=0)
+
+    hsel, gsel = picked(hid_t), picked(hgr_t)
+
+    def outer(dst, start, stop):
+        for lo in range(start, stop, 512):
+            hi = min(lo + 512, stop)
+            left = jnp.dot(hsel, pg[:, lo:hi], preferred_element_type=f32)
+            right = jnp.dot(gsel[:, :samples], ci_ref[:, lo:hi], preferred_element_type=f32)
+            right += jnp.dot(gsel[:, samples:], ci2[:, lo:hi], preferred_element_type=f32)
+            for d in range(2 * n_tbl):
+                both = jnp.concatenate([left[8 * d : 8 * d + 8], right[8 * d : 8 * d + 8]], axis=0)
+                tt = d % n_tbl
+                dst[d // n_tbl, tt // 4, (tt // 2) % 2, tt % 2, :, lo - start : hi - start] = (
+                    both.astype(bf16)
+                )
+
+    outer(sa, 0, cut)
+    a1 = send(sa.at[1 - x], ra1, ssem.at[0], rsem.at[0], xg, t)
+    outer(sb, cut, width)
+    b1 = send(sb.at[:, :, :, 1 - y], rb1, ssem.at[1], rsem.at[1], g, yt)
+
+    mine.wait()
+    for copy in id_copies:
+        copy.wait()
+
+    index = lax.broadcasted_iota(jnp.int32, (2 * part, samples), 0)
+    row_of = (index // part * 2 + core) * part + index % part
+
+    def tables(pair, carry):
+        base = pl.multiple_of(EMB + pair * 2 * EMB, EMB)
+        cols = pl.ds(base, 2 * EMB)
+        mixed = jnp.dot(hid[...], u_ref[:, cols], preferred_element_type=f32) + bias_ref[:, cols]
+        back = jnp.dot(hgr[...], v_ref[:, cols], preferred_element_type=f32)
+        up_all = jnp.concatenate([up_ref[:, cols], up2[:, cols]], axis=0).astype(f32)
+        pooled = (up_all * (1.0 + mixed) + back).astype(bf16)
+        for half in range(2):
+            table = pair * 2 + half
+            owner, slot = place_ref[0, table], place_ref[1, table]
+            sums = jnp.zeros((2 * part, EMB), f32)
+            for who in range(2):
+                looked = ids_in[who, owner, slot]
+                count = jnp.zeros((2 * part, samples), f32)
+                for k in range(looked.shape[0]):
+                    count += jnp.where(looked[k : k + 1, :] == row_of, 1.0, 0.0)
+                sums += jnp.dot(
+                    count.astype(bf16),
+                    pooled[who * samples : (who + 1) * samples, half * EMB : (half + 1) * EMB],
+                    preferred_element_type=f32,
+                )
+            st[0, table] = sums[:part].astype(bf16)
+            st[1, table] = sums[part:].astype(bf16)
+        return carry
+
+    def plus(p, q):
+        return p.astype(f32) + q.astype(f32)
+
+    half_pairs = TABLES // 4
+    lax.fori_loop(0, half_pairs, tables, 0)
+
+    a1.wait()
+    for i in range(2):
+        for j in range(2):
+            for k in range(2):
+                pa1[i, j, k] = plus(sa[x, i, j, k], ra1[i, j, k]).astype(bf16)
+    a2 = send(pa1.at[:, :, 1 - y], ra2, ssem.at[2], rsem.at[2], g, yt)
+
+    lax.fori_loop(half_pairs, TABLES // 2, tables, 0)
+    t1 = send(st.at[1 - x], rt1, ssem.at[3], rsem.at[3], xg, t)
+
+    b1.wait()
+    for i in range(2):
+        for j in range(2):
+            for k in range(2):
+                pb1[i, j, k] = plus(sb[i, j, k, y], rb1[i, j, k]).astype(bf16)
+    b2 = send(pb1.at[1 - x], rb2, ssem.at[4], rsem.at[4], xg, t)
+
+    a2.wait()
+    for i in range(2):
+        for j in range(2):
+            pa2[i, j] = plus(pa1[i, j, y], ra2[i, j]).astype(bf16)
+    a3 = send(pa2.at[:, 1 - zl], ra3, ssem.at[5], rsem.at[5], g, zlt)
+
+    t1.wait()
+
+    def add_table(i, carry):
+        pt1[i] = plus(st[x, i], rt1[i])
+        return carry
+
+    lax.fori_loop(0, TABLES, add_table, 0)
+
+    def expand(i, carry):
+        which = inv_ref[i]
+        there = jnp.where(which >= 0, 1.0, 0.0)
+        owner, slot = i // slots_dev, i % slots_dev
+        pte[owner // 4, (owner // 2) % 2, owner % 2, slot] = (
+            pt1[jnp.maximum(which, 0)] * there
+        ).astype(bf16)
+        return carry
+
+    lax.fori_loop(0, slots_dev * n_tbl, expand, 0)
+    t2 = send(pte.at[:, :, 1 - y], rt2, ssem.at[6], rsem.at[6], g, yt)
+
+    b2.wait()
+    for i in range(2):
+        for j in range(2):
+            pb2[i, j] = plus(pb1[x, i, j], rb2[i, j]).astype(bf16)
+    b3 = send(pb2.at[:, 1 - zl], rb3, ssem.at[7], rsem.at[7], g, zlt)
+
+    a3.wait()
+    for i in range(2):
+        pa3[i] = plus(pa2[i, zl], ra3[i]).astype(bf16)
+    a4 = send(pa3.at[1 - zh], ra4, ssem.at[8], rsem.at[8], g, zht)
+
+    b3.wait()
+    for i in range(2):
+        pb3[i] = plus(pb2[i, zl], rb3[i]).astype(bf16)
+    b4 = send(pb3.at[1 - zh], rb4, ssem.at[9], rsem.at[9], g, zht)
+
+    t2.wait()
+    for i in range(2):
+        for j in range(2):
+            pt2[i, j] = plus(pte[i, j, y], rt2[i, j]).astype(bf16)
+    t3 = send(pt2.at[:, 1 - zl], rt3, ssem.at[10], rsem.at[10], g, zlt)
+
+    def finish(value, lo, hi):
+        value = value * scale
+        cross_ref[:, lo:hi] = value[:8]
+        cross_ref[:, width + lo : width + hi] = value[8:]
+
+    a4.wait()
+    finish(plus(pa3[zh], ra4[...]), 0, cut)
+    b4.wait()
+    finish(plus(pb3[zh], rb4[...]), cut, width)
+    t3.wait()
+    for i in range(2):
+        pt3[i] = plus(pt2[i, zl], rt3[i]).astype(bf16)
+    t4 = send(pt3.at[1 - zh], rt4, ssem.at[11], rsem.at[11], g, zht)
+    t4.wait()
+    table_ref[...] = plus(pt3[zh], rt4[...])
+
+
+def on_device_fused(cross_input, upstream, v_weight, u_weight, bias, placement, owned_ids):
+    n_grp = lax.axis_size("grp")
+    n_tbl = lax.axis_size("tbl")
+    samples, width = cross_input.shape
+    rank = v_weight.shape[0]
+    slots_dev, hot = owned_ids.shape[:2]
+    scale = 1.0 / math.sqrt(samples * n_grp * n_tbl)
+    order = jnp.arange(TABLES, dtype=jnp.int32)
+    same = placement[:, None] == placement[None, :]
+    slot = jnp.sum((same & (order[None, :] < order[:, None])).astype(jnp.int32), axis=1)
+    places = jnp.stack([placement, slot])
+    hit = jnp.arange(slots_dev * n_tbl, dtype=jnp.int32)[:, None] == (placement * slots_dev + slot)
+    inverse = jnp.max(jnp.where(hit, order[None, :], -1), axis=1)
+    part = ROWS // n_grp
+    cut = (width // EMB * 2 // 5) * EMB
+    rest = width - cut
+    bf16, f32, i32 = jnp.bfloat16, jnp.float32, jnp.int32
+    V = pltpu.VMEM
+    tab = (slots_dev, part, EMB)
+    scratch = [
+        V((samples, width), bf16), V((samples, width), bf16), V((2 * samples, width), bf16),
+        V((2 * samples, rank), bf16), V((2 * samples, rank), bf16),
+        V((rank, 2 * samples), bf16), V((rank, 2 * samples), bf16),
+        V((2, n_tbl, slots_dev, hot, samples), i32),
+        V((2, 2, 2, 2, 16, cut), bf16), V((2, 2, 2, 2, 16, rest), bf16),
+        V((2, TABLES, part, EMB), bf16),
+        V((2, 2, 2, 16, cut), bf16), V((2, 2, 16, cut), bf16), V((2, 16, cut), bf16), V((16, cut), bf16),
+        V((2, 2, 2, 16, rest), bf16), V((2, 2, 16, rest), bf16), V((2, 16, rest), bf16), V((16, rest), bf16),
+        V((TABLES, part, EMB), bf16), V((2, 2, *tab), bf16), V((2, *tab), bf16), V(tab, bf16),
+        V((2, 2, 2, 16, cut), bf16), V((2, 2, 16, cut), bf16), V((2, 16, cut), bf16),
+        V((2, 2, 2, 16, rest), bf16), V((2, 2, 16, rest), bf16), V((2, 16, rest), bf16),
+        V((TABLES, part, EMB), f32), V((2, 2, 2, *tab), bf16), V((2, 2, *tab), bf16), V((2, *tab), bf16),
+        pltpu.SemaphoreType.DMA((12,)), pltpu.SemaphoreType.DMA((12,)),
+        pltpu.SemaphoreType.DMA((2,)), pltpu.SemaphoreType.DMA((2,)),
+        pltpu.SemaphoreType.DMA((2, n_tbl)), pltpu.SemaphoreType.DMA((2, n_tbl)),
+    ]
+    vmem = pl.BlockSpec(memory_space=pltpu.VMEM)
+    smem = pl.BlockSpec(memory_space=pltpu.SMEM)
+    return pl.pallas_call(
+        functools.partial(fused_body, n_grp, n_tbl, scale, cut),
+        out_shape=(
+            jax.ShapeDtypeStruct((2 * rank // (n_grp * n_tbl) // 2, 2 * width), f32),
+            jax.ShapeDtypeStruct(tab, f32),
+        ),
+        in_specs=[vmem] * 5 + [smem] * 2 + [vmem],
+        out_specs=(vmem, vmem),
+        scratch_shapes=scratch,
+        compiler_params=pltpu.CompilerParams(
+            collective_id=0, has_side_effects=True, vmem_limit_bytes=60 * 1024 * 1024
+        ),
+        name="cross_backward",
+    )(cross_input, upstream, v_weight, u_weight, bias[None, :], places, inverse, owned_ids)
 
 
 def solution(mesh):
@@ -69,6 +358,8 @@
         P("tbl", None, "grp"),
     )
     out_specs = (P(("grp", "tbl"), None), P("tbl", "grp", None))
+    sizes = mesh.shape
+    fused = flip_stages(sizes["grp"], sizes["tbl"])
     return jax.shard_map(
-        on_device, mesh=mesh, in_specs=in_specs, out_specs=out_specs, check_vma=False
-    )
+        on_device_fused if fused else on_device, mesh=mesh, in_specs=in_specs, out_specs=out_specs, check_vma=False
+    )

time: 170 us -> 67.8 us (0.40)
  waiting for transfers between devices: 121 us -> 0 us
  Pallas kernels: 0 us -> 58.9 us
  between operations: 14.2 us -> 0.64 us
  matrix products: 8.03 us -> 0 us
  starting transfers between devices: 7.52 us -> 0 us
  other arithmetic: 10.4 us -> 3.46 us
  local copies, waits for them, and re-layouts: 8.59 us -> 4.55 us
    reduce_scatter x2 -> x0, waiting for transfers between devices: 94.6 us -> none  [the longest x1 71.8 us: on_device(): lax.psum_scatter(term, ('grp', 'tbl'), scatter_dimension=0, tiled=True)]
    pallas_call x0 -> x1, Pallas kernels: none -> 58.9 us  [on_device_fused(): pl.pallas_call(functools.partial(fused_body, n_grp, n_tbl, scale, cut), o...]
    all_to_all x1 -> x0, waiting for transfers between devices: 26.5 us -> none  [on_device(): lax.all_to_all(outgoing, 'tbl', split_axis=1, concat_axis=1, tiled=True)]
    dot_general x8 -> x0, matrix products: 8.03 us -> none  [the longest x1 2.89 us: on_device(): jnp.dot(product_grad, u_weight.T, preferred_element_type=jnp.float32)]
    all_to_all x1 -> x0, starting transfers between devices: 7.44 us -> none  [on_device(): lax.all_to_all(outgoing, 'tbl', split_axis=1, concat_axis=1, tiled=True)]
    reduce_sum x2 -> x1, other arithmetic: 4.99 us -> 0.91 us  [on_device_fused(): jnp.sum((same & (order[None, :] < order[:, None])).astype(jnp.int32), axi...]
    concatenate x1 -> x0, other arithmetic: 3.39 us -> none  [on_device(): jnp.concatenate([outer_sum(hidden, product_grad), outer_sum(hidden_grad,...]
    reshape x2 -> x0, local copies, waits for them, and re-layouts: 3.32 us -> none  [the longest x1 1.93 us: on_device(): input_grad[:, EMB:].astype(jnp.bfloat16).reshape(samples, TABLES, EMB)]
  transfers between devices with their start and end apart: 3 -> 0, of which waited for: 3 -> 0; matrix products, arithmetic and copies ran while one was open for 9% -> 0% of each run, Pallas kernels for 0% -> 0%
where the time goes in v1:
time: 67.8 us; the launch traced here: 67.5 us
  Pallas kernels  58.9 us (87%)
  local copies, waits for them, and re-layouts  4.55 us (7%)
  other arithmetic  3.46 us (5%)
    pallas_call x1, Pallas kernels, on_device_fused(): pl.pallas_call(functools.partial(fused_body, n_grp, n_tbl, scale, cut), o...  58.9 us
    unnamed x2, local copies, waits for them, and re-layouts  3.23 us

profile of v1, /device:TPU:0, one launch (start us, length us, event | category | flops | bytes accessed | tf_op | source)
XLA Modules:
  0.0 67.5 jit_solution(3701394258405497745)
XLA Ops:
  0.6 0.9 %convert_reduce_fusion = s32[26]{0:T(128)S(1)} fusion(s32[26]{0:T(128)} %param.12), kind=kLoop, calls=%fused_computation.2 | loop fusion | flops 3354 | bytes 208 | tf_op jit(solution)/shard_map/reduce_sum | solution.py:305
  1.5 0.7 multiply_add_fusion
  2.2 0.7 select_reduce_fusion.inv_ref
  2.9 1.2 %pad_add_fusion.place_ref = s32[2,26]{1,0:T(2,128)} fusion(s32[1,26]{1,0:T(1,128)S(1)} %bitcast.3, s32[1,26]{1,0:T(1,128)} %bitcast.2), kind=kLoop, calls=%fused_computation.5 | loop fusion | flops 52 | bytes 416 | tf_op jit(solution)/shard_map/stack | solution.py:306
  4.1 1.3 %broadcast_in_dim.10.bias_ref = f32[1,3456]{1,0:T(1,128)} reshape(f32[3456]{0:T(1024)} %param.11) | data formatting | bytes 27648 | tf_op jit(solution)/shard_map/broadcast_in_dim | solution.py:347
  5.4 58.9 %cross_backward.1 = (f32[8,6912]{1,0:T(8,128)}, f32[5,64,128]{2,1,0:T(8,128)}) custom-call(bf16[128,3456]{1,0:T(8,128)(2,1)} %ci_ref.1, bf16[128,3456]{1,0:T(8,128)(2,1)} %up_ref.1, bf16[256,3456]{1,0:T(8,128)(2,1)} %v_ref.1, bf16[256,3456]{1,0:T(8,128)(2,1)} %u_ref.1, f32[1,3456]{1,0:T(1,128)} %broadcast_in_dim.10.bias_ref, s32[2,26]{1,0:T(2,128)} %pad_add_fusion.place_ref, ...), custom_call_target="tpu_custom_call" | custom-call | tf_op jit(solution)/shard_map/cross_backward/pallas_call | solution.py:334
  64.3 1.6 %copy.11 = f32[8,6912]{1,0:T(8,128)} copy(f32[8,6912]{1,0:T(8,128)} %get-tuple-element.4) | data formatting | bytes 442368
  65.9 1.6 %copy.12 = f32[5,64,128]{2,1,0:T(8,128)} copy(f32[5,64,128]{2,1,0:T(8,128)} %get-tuple-element.5) | data formatting | bytes 327680

commit v2 on v0

--- a/solution.py
+++ b/solution.py
@@ -1,13 +1,17 @@
+import functools
 import math
 
 import jax
 import jax.numpy as jnp
 from jax import lax
+from jax.experimental import pallas as pl
+from jax.experimental.pallas import tpu as pltpu
 from jax.sharding import PartitionSpec as P
 
 EMB = 128
 TABLES = 26
 ROWS = 256
+MESH = pl.DeviceIdType.MESH
 
 
 def outer_sum(left, right):
@@ -56,6 +60,382 @@
     summed = lax.psum_scatter(term, ("grp", "tbl"), scatter_dimension=0, tiled=True)
     cross_grad = summed * scale
     return (cross_grad, table_grad)
+
+
+def halving_fits(n_grp, n_tbl):
+    return n_grp == 4 and n_tbl == 8
+
+
+def scratch_of(samples, width, rank, n_tbl, slots_dev, hot, part, cut):
+    f32, bf16, i32 = jnp.float32, jnp.bfloat16, jnp.int32
+    V, rest, half = pltpu.VMEM, width - cut, part // 2
+    tab = (slots_dev, half, EMB)
+    out = {
+        "ci": V((2, samples, width), bf16),
+        "up": V((2, samples, width), bf16),
+        "v": V((rank, width), bf16),
+        "u": V((rank, width), bf16),
+        "pg": V((2 * samples, width), bf16),
+        "hid": V((2 * samples, rank), bf16),
+        "hgr": V((2 * samples, rank), bf16),
+        "hid_t": V((rank, 2 * samples), bf16),
+        "hgr_t": V((rank, 2 * samples), bf16),
+        "ids": V((2, n_tbl, slots_dev, hot, samples), i32),
+        "pt": V((2, TABLES, half, EMB), f32),
+        "slot": pltpu.SMEM((TABLES,), i32),
+        "inv": pltpu.SMEM((slots_dev * n_tbl,), i32),
+        "load_sem": pltpu.SemaphoreType.DMA((4,)),
+        "in_s": pltpu.SemaphoreType.DMA((2,)),
+        "in_r": pltpu.SemaphoreType.DMA((2,)),
+        "id_s": pltpu.SemaphoreType.DMA((2, n_tbl)),
+        "id_r": pltpu.SemaphoreType.DMA((2, n_tbl)),
+        "ssem": pltpu.SemaphoreType.DMA((16,)),
+        "rsem": pltpu.SemaphoreType.DMA((16,)),
+    }
+    lead = ((2, 2, 2), (2, 2), (2,), ())
+    for name, first, tile in (
+        ("a", (2, 2, 2), (16, cut)),
+        ("b", (2, 2, 2), (16, rest)),
+        ("c", None, tab),
+        ("d", (2, 2, 2), tab),
+    ):
+        for k in range(4):
+            shape = lead[k] + tile
+            if name == "c" and k == 0:
+                shape = (TABLES, half, EMB)
+            out["s%s%d" % (name, k)] = V(shape, bf16)
+            out["r%s%d" % (name, k)] = V(shape, bf16)
+            out["o%s%d" % (name, k)] = V(shape, f32)
+    return out
+
+
+def fused_body(n_grp, n_tbl, scale, cut, names, *refs):
+    f32, bf16 = jnp.float32, jnp.bfloat16
+    ci_hbm, up_hbm, v_hbm, u_hbm, bias_ref, place_ref, ids_hbm, cross_ref, table_ref = refs[:9]
+    r = dict(zip(names, refs[9:]))
+    g = lax.axis_index("grp")
+    t = lax.axis_index("tbl")
+    core, x = g % 2, g // 2
+    y, zl, zh = t % 2, (t // 2) % 2, t // 4
+    og = g + 1 - 2 * core
+    xg = core + 2 * (1 - x)
+    yt = t + 1 - 2 * y
+    zlt = t + 2 * (1 - 2 * zl)
+    zht = t + 4 * (1 - 2 * zh)
+    samples, width = ci_hbm.shape
+    rank = v_hbm.shape[0]
+    slots_dev = ids_hbm.shape[0]
+    part = ROWS // n_grp
+    half = part // 2
+
+    barrier = pltpu.get_barrier_semaphore()
+
+    def greet(gg, tt):
+        pl.semaphore_signal(barrier, inc=1, device_id=(gg, tt), device_id_type=MESH)
+
+    for step in range(1, n_tbl):
+        greet(g, (t + step) % n_tbl)
+        greet(og, (t + step) % n_tbl)
+    greet(og, t)
+    greet(xg, t)
+
+    loads = [
+        pltpu.make_async_copy(src, dst, r["load_sem"].at[i])
+        for i, (src, dst) in enumerate(
+            ((ci_hbm, r["ci"].at[0]), (v_hbm, r["v"]), (up_hbm, r["up"].at[0]), (u_hbm, r["u"]))
+        )
+    ]
+    for load in loads:
+        load.start()
+
+    places = [place_ref[i] for i in range(TABLES)]
+    targets = []
+    for i in range(TABLES):
+        slot = jnp.int32(0)
+        for j in range(i):
+            slot += (places[j] == places[i]).astype(jnp.int32)
+        r["slot"][i] = jnp.minimum(slot, slots_dev - 1)
+        targets.append(places[i] * slots_dev + slot)
+    for q in range(slots_dev * n_tbl):
+        which = jnp.int32(-1)
+        for i in range(TABLES):
+            which = jnp.where(targets[i] == q, i, which)
+        r["inv"][q] = which
+
+    pl.semaphore_wait(barrier, 2 * n_tbl)
+
+    def remote(src, dst, s, rs, gg, tt):
+        copy = pltpu.make_async_remote_copy(
+            src_ref=src, dst_ref=dst, send_sem=s, recv_sem=rs,
+            device_id=(gg, tt), device_id_type=MESH,
+        )
+        copy.start()
+        return copy
+
+    in_copies = [
+        remote(ci_hbm, r["ci"].at[1], r["in_s"].at[0], r["in_r"].at[0], og, t),
+        remote(up_hbm, r["up"].at[1], r["in_s"].at[1], r["in_r"].at[1], og, t),
+    ]
+    id_copies = []
+    for step in range(n_tbl):
+        to = (t + step) % n_tbl
+        block = ids_hbm.at[:, :, pl.ds(pl.multiple_of(to * samples, samples), samples)]
+        if step == 0:
+            mine = pltpu.make_async_copy(block, r["ids"].at[0, t], r["id_s"].at[0, 0])
+            mine.start()
+        else:
+            id_copies.append(
+                remote(block, r["ids"].at[0, t], r["id_s"].at[0, step], r["id_r"].at[0, step], g, to)
+            )
+        id_copies.append(
+            remote(block, r["ids"].at[1, t], r["id_s"].at[1, step], r["id_r"].at[1, step], og, to)
+        )
+
+    nt = (((1,), (1,)), ((), ()))
+
+    def forward(who):
+        row = who * samples
+        rows = pl.ds(row, samples)
+        if who == 0:
+            loads[0].wait()
+            loads[1].wait()
+        else:
+            in_copies[0].wait()
+        hidden = lax.dot_general(r["ci"][who], r["v"][...], nt, preferred_element_type=f32)
+        r["hid"][rows, :] = hidden.astype(bf16)
+        r["hid_t"][:, rows] = hidden.T.astype(bf16)
+        if who == 0:
+            loads[2].wait()
+            loads[3].wait()
+        else:
+            in_copies[1].wait()
+        r["pg"][rows, :] = (r["up"][who].astype(f32) * r["ci"][who].astype(f32)).astype(bf16)
+        hgrad = lax.dot_general(r["pg"][rows, :], r["u"][...], nt, preferred_element_type=f32)
+        r["hgr"][rows, :] = hgrad.astype(bf16)
+        r["hgr_t"][:, rows] = hgrad.T.astype(bf16)
+
+    forward(0)
+    forward(1)
+
+    quarter = rank // n_grp
+
+    def picked(ref):
+        mine_rows = ref[pl.ds(pl.multiple_of((core + 2 * x) * quarter, quarter), quarter), :]
+        other_rows = ref[pl.ds(pl.multiple_of((core + 2 - 2 * x) * quarter, quarter), quarter), :]
+        return jnp.concatenate([mine_rows, other_rows], axis=0)
+
+    hsel, gsel = picked(r["hid_t"]), picked(r["hgr_t"])
+
+    def blocks(lo, hi):
+        left = jnp.dot(hsel, r["pg"][:, lo:hi], preferred_element_type=f32)
+        right = jnp.dot(gsel[:, :samples], r["ci"][0, :, lo:hi], preferred_element_type=f32)
+        right += jnp.dot(gsel[:, samples:], r["ci"][1, :, lo:hi], preferred_element_type=f32)
+        return [
+            jnp.concatenate([left[8 * d : 8 * d + 8], right[8 * d : 8 * d + 8]], axis=0)
+            for d in range(2 * n_tbl)
+        ]
+
+    for lo in range(0, cut, 512):
+        hi = min(lo + 512, cut)
+        made = blocks(lo, hi)
+        for d in range(n_tbl):
+            at = (d // 4, (d // 2) % 2, d % 2, slice(None), slice(lo, hi))
+            r["oa0"][at] = made[d]
+            r["sa0"][at] = made[n_tbl + d].astype(bf16)
+    sems = iter(range(16))
+
+    def send(name, k, gg, tt):
+        i = next(sems)
+        return remote(
+            r["s%s%d" % (name, k)], r["r%s%d" % (name, k)], r["ssem"].at[i], r["rsem"].at[i], gg, tt
+        )
+
+    a0 = send("a", 0, xg, t)
+    for lo in range(cut, width, 512):
+        hi = min(lo + 512, width)
+        made = blocks(lo, hi)
+        for side in range(2):
+            xx = x if side == 0 else 1 - x
+            for z in range(n_tbl // 2):
+                even, odd = made[side * n_tbl + 2 * z], made[side * n_tbl + 2 * z + 1]
+                at = (xx, z // 2, z % 2, slice(None), slice(lo - cut, hi - cut))
+                r["ob0"][at] = jnp.where(y == 0, even, odd)
+                r["sb0"][at] = jnp.where(y == 0, odd, even).astype(bf16)
+    b0 = send("b", 0, g, yt)
+
+    def indices(depth):
+        out = [()]
+        for _ in range(depth):
+            out = [i + (j,) for i in out for j in range(2)]
+        return out
+
+    def halve(name, k, axis, bit, gg, tt, before):
+        before.wait()
+        own, came = r["o%s%d" % (name, k)], r["r%s%d" % (name, k)]
+        kept, out = r["o%s%d" % (name, k + 1)], r["s%s%d" % (name, k + 1)]
+
+        def where_to(i, b):
+            return i[:axis] + (b,) + i[axis:]
+
+        def fill(dst, b, kind):
+            for i in indices(2 - k):
+                at = where_to(i, b)
+                value = own[at] + came[at].astype(f32)
+                if i:
+                    dst[i] = value.astype(kind)
+                else:
+                    dst[...] = value.astype(kind)
+
+        fill(out, 1 - bit, bf16)
+        copy = send(name, k + 1, gg, tt)
+        fill(kept, bit, f32)
+        return copy
+
+    index = lax.broadcasted_iota(jnp.int32, (2 * part, samples), 0)
+    side_of = jnp.where(index // part == 0, x, 1 - x)
+    row_of = (side_of * 2 + core) * part + index % part
+
+    def tables(pair, carry):
+        cols = pl.ds(pl.multiple_of(EMB + pair * 2 * EMB, EMB), 2 * EMB)
+        shift = jnp.concatenate(
+            [bias_ref[pl.ds(1 + 2 * pair, 1), :], bias_ref[pl.ds(2 + 2 * pair, 1), :]], axis=1
+        )
+        mixed = jnp.dot(r["hid"][...], r["u"][:, cols], preferred_element_type=f32) + shift
+        back = jnp.dot(r["hgr"][...], r["v"][:, cols], preferred_element_type=f32)
+        up_all = jnp.concatenate([r["up"][0, :, cols], r["up"][1, :, cols]], axis=0).astype(f32)
+        pooled = (up_all * (1.0 + mixed) + back).astype(bf16)
+        for piece in range(2):
+            table = pair * 2 + piece
+            owner, slot = place_ref[table], r["slot"][table]
+            sums = jnp.zeros((2 * part, EMB), f32)
+            for who in range(2):
+                looked = r["ids"][who, owner, slot]
+                count = jnp.zeros((2 * part, samples), f32)
+                for k in range(looked.shape[0]):
+                    count += jnp.where(looked[k : k + 1, :] == row_of, 1.0, 0.0)
+                sums += jnp.dot(
+                    count.astype(bf16),
+                    pooled[who * samples : (who + 1) * samples, piece * EMB : (piece + 1) * EMB],
+                    preferred_element_type=f32,
+                )
+            r["oc0"][table] = sums[:half]
+            r["sc0"][table] = sums[part : part + half].astype(bf16)
+            r["pt"][x, table] = sums[half:part]
+            r["pt"][1 - x, table] = sums[part + half :]
+        return carry
+
+    mine.wait()
+    for copy in id_copies:
+        copy.wait()
+    early = TABLES // 4
+    lax.fori_loop(0, early, tables, 0)
+    a1 = halve("a", 0, 2, y, g, yt, a0)
+    lax.fori_loop(early, TABLES // 2, tables, 0)
+    c0 = send("c", 0, xg, t)
+
+    def each_slot(yy, put):
+        def run(i, carry):
+            owner = i // slots_dev * 2 + yy
+            which = r["inv"][owner * slots_dev + i % slots_dev]
+            there = jnp.where(which >= 0, 1.0, 0.0)
+            z = i // slots_dev
+            put((z // 2, z % 2, i % slots_dev), jnp.maximum(which, 0), there)
+            return carry
+
+        lax.fori_loop(0, slots_dev * n_tbl // 2, run, 0)
+
+    def put_d(ref, kind):
+        def put(at, which, there):
+            for xx in range(2):
+                ref[(xx, *at)] = (r["pt"][xx, which] * there).astype(kind)
+
+        return put
+
+    def put_c(ref, kind):
+        def put(at, which, there):
+            ref[at] = ((r["oc0"][which] + r["rc0"][which].astype(f32)) * there).astype(kind)
+
+        return put
+
+    each_slot(1 - y, put_d(r["sd0"], bf16))
+    d0 = send("d", 0, g, yt)
+    b1 = halve("b", 0, 0, x, xg, t, b0)
+    each_slot(y, put_d(r["od0"], f32))
+    a2 = halve("a", 1, 1, zl, g, zlt, a1)
+    c0.wait()
+    each_slot(1 - y, put_c(r["sc1"], bf16))
+    c1 = send("c", 1, g, yt)
+    each_slot(y, put_c(r["oc1"], f32))
+    d1 = halve("d", 0, 0, x, xg, t, d0)
+    a3 = halve("a", 2, 0, zh, g, zht, a2)
+    b2 = halve("b", 1, 1, zl, g, zlt, b1)
+    c2 = halve("c", 1, 1, zl, g, zlt, c1)
+    d2 = halve("d", 1, 1, zl, g, zlt, d1)
+    b3 = halve("b", 2, 0, zh, g, zht, b2)
+    c3 = halve("c", 2, 0, zh, g, zht, c2)
+    d3 = halve("d", 2, 0, zh, g, zht, d2)
+
+    def total(name):
+        return r["o%s3" % name][...] + r["r%s3" % name][...].astype(f32)
+
+    def finish(value, lo, hi):
+        value = value * scale
+        cross_ref[:, lo:hi] = value[:8]
+        cross_ref[:, width + lo : width + hi] = value[8:]
+
+    a3.wait()
+    finish(total("a"), 0, cut)
+    b3.wait()
+    finish(total("b"), cut, width)
+    c3.wait()
+    table_ref[:, :half, :] = total("c")
+    d3.wait()
+    table_ref[:, half:, :] = total("d")
+
+
+def copy_body(cross_ref, table_ref, cross_out, table_out):
+    cross_out[...] = cross_ref[...]
+    table_out[...] = table_ref[...]
+
+
+def on_device_fused(cross_input, upstream, v_weight, u_weight, bias, placement, owned_ids):
+    n_grp = lax.axis_size("grp")
+    n_tbl = lax.axis_size("tbl")
+    samples, width = cross_input.shape
+    rank = v_weight.shape[0]
+    slots_dev, hot = owned_ids.shape[:2]
+    scale = 1.0 / math.sqrt(samples * n_grp * n_tbl)
+    part = ROWS // n_grp
+    cut = (width // EMB // 2) * EMB
+    scratch = scratch_of(samples, width, rank, n_tbl, slots_dev, hot, part, cut)
+    vmem = pl.BlockSpec(memory_space=pltpu.VMEM)
+    smem = pl.BlockSpec(memory_space=pltpu.SMEM)
+    hbm = pl.BlockSpec(memory_space=pl.ANY)
+    shapes = (
+        jax.ShapeDtypeStruct((rank // (n_grp * n_tbl), 2 * width), jnp.float32),
+        jax.ShapeDtypeStruct((slots_dev, part, EMB), jnp.float32),
+    )
+    sums = pl.pallas_call(
+        functools.partial(fused_body, n_grp, n_tbl, scale, cut, tuple(scratch)),
+        out_shape=shapes,
+        in_specs=[hbm] * 4 + [vmem, smem, hbm],
+        out_specs=(vmem, vmem),
+        scratch_shapes=list(scratch.values()),
+        compiler_params=pltpu.CompilerParams(
+            collective_id=0, has_side_effects=True, vmem_limit_bytes=60 * 1024 * 1024
+        ),
+        name="cross_backward",
+    )(
+        cross_input, upstream, v_weight, u_weight,
+        bias.reshape(width // EMB, EMB), placement, owned_ids,
+    )
+    return pl.pallas_call(
+        copy_body,
+        out_shape=shapes,
+        in_specs=[vmem, vmem],
+        out_specs=(vmem, vmem),
+        name="hand_over",
+    )(*sums)
 
 
 def solution(mesh):
@@ -69,6 +449,7 @@
         P("tbl", None, "grp"),
     )
     out_specs = (P(("grp", "tbl"), None), P("tbl", "grp", None))
+    fused = halving_fits(mesh.shape["grp"], mesh.shape["tbl"])
     return jax.shard_map(
-        on_device, mesh=mesh, in_specs=in_specs, out_specs=out_specs, check_vma=False
-    )
+        on_device_fused if fused else on_device, mesh=mesh, in_specs=in_specs, out_specs=out_specs, check_vma=False
+    )

time: 170 us -> 54.5 us (0.32)
  waiting for transfers between devices: 121 us -> 0 us
  Pallas kernels: 0 us -> 53.6 us
  between operations: 14.2 us -> 0.64 us
  other arithmetic: 10.4 us -> 0 us
  local copies, waits for them, and re-layouts: 8.59 us -> 0 us
  matrix products: 8.03 us -> 0 us
  starting transfers between devices: 7.52 us -> 0 us
    reduce_scatter x2 -> x0, waiting for transfers between devices: 94.6 us -> none  [the longest x1 71.8 us: on_device(): lax.psum_scatter(term, ('grp', 'tbl'), scatter_dimension=0, tiled=True)]
    pallas_call x0 -> x2, Pallas kernels: none -> 53.6 us  [the longest x1 51.8 us: on_device_fused(): pl.pallas_call(functools.partial(fused_body, n_grp, n_tbl, scale, cut, tu...]
    all_to_all x1 -> x0, waiting for transfers between devices: 26.5 us -> none  [on_device(): lax.all_to_all(outgoing, 'tbl', split_axis=1, concat_axis=1, tiled=True)]
    dot_general x8 -> x0, matrix products: 8.03 us -> none  [the longest x1 2.89 us: on_device(): jnp.dot(product_grad, u_weight.T, preferred_element_type=jnp.float32)]
    all_to_all x1 -> x0, starting transfers between devices: 7.44 us -> none  [on_device(): lax.all_to_all(outgoing, 'tbl', split_axis=1, concat_axis=1, tiled=True)]
    reduce_sum x2 -> x0, other arithmetic: 4.99 us -> none  [the longest x1 4.81 us: on_device(): jnp.sum((owned_ids[:, :, None, :] == row_numbers[None, None, :, None]).as...]
    unnamed x24 -> x0, local copies, waits for them, and re-layouts: 3.86 us -> none
    concatenate x1 -> x0, other arithmetic: 3.39 us -> none  [on_device(): jnp.concatenate([outer_sum(hidden, product_grad), outer_sum(hidden_grad,...]
  transfers between devices with their start and end apart: 3 -> 0, of which waited for: 3 -> 0; matrix products, arithmetic and copies ran while one was open for 9% -> 0% of each run, Pallas kernels for 0% -> 0%
where the time goes in v2:
time: 54.5 us; the launch traced here: 54.2 us
  Pallas kernels  53.6 us (98%)
  between operations  0.64 us (1%)
    pallas_call x1, Pallas kernels, on_device_fused(): pl.pallas_call(functools.partial(fused_body, n_grp, n_tbl, scale, cut, tu...  51.8 us
    pallas_call x1, Pallas kernels, on_device_fused(): pl.pallas_call(copy_body, out_shape=shapes, in_specs=[vmem, vmem], out_sp...  1.78 us

profile of v2, /device:TPU:0, one launch (start us, length us, event | category | flops | bytes accessed | tf_op | source)
XLA Modules:
  0.0 54.2 jit_solution(5898015987549872280)
XLA Ops:
  0.6 51.8 %cross_backward.1 = (f32[8,6912]{1,0:T(8,128)}, f32[5,64,128]{2,1,0:T(8,128)}) custom-call(bf16[128,3456]{1,0:T(8,128)(2,1)} %refs_0_.1, bf16[128,3456]{1,0:T(8,128)(2,1)} %refs_1_.1, bf16[256,3456]{1,0:T(8,128)(2,1)} %refs_2_.1, bf16[256,3456]{1,0:T(8,128)(2,1)} %refs_3_.1, f32[27,128]{1,0:T(8,128)} %bitcast.1, s32[26]{0:T(128)} %refs_5_.1, ...), custom_call_target="tpu_custom_call" | custom-call | tf_op jit(solution)/shard_map/cross_backward/pallas_call | solution.py:418
  52.4 1.8 %hand_over.1 = (f32[8,6912]{1,0:T(8,128)}, f32[5,64,128]{2,1,0:T(8,128)}) custom-call(f32[8,6912]{1,0:T(8,128)} %get-tuple-element.4.cross_ref, f32[5,64,128]{2,1,0:T(8,128)} %get-tuple-element.5.table_ref), custom_call_target="tpu_custom_call" | custom-call | tf_op jit(solution)/shard_map/hand_over/pallas_call | solution.py:432

commit v3 on v2

--- a/solution.py
+++ b/solution.py
@@ -66,42 +66,42 @@
     return n_grp == 4 and n_tbl == 8
 
 
-def scratch_of(samples, width, rank, n_tbl, slots_dev, hot, part, cut):
+def scratch_of(samples, width, rank, n_tbl, slots_dev, hot, part, cuts):
     f32, bf16, i32 = jnp.float32, jnp.bfloat16, jnp.int32
-    V, rest, half = pltpu.VMEM, width - cut, part // 2
+    V, half = pltpu.VMEM, part // 2
     tab = (slots_dev, half, EMB)
     out = {
         "ci": V((2, samples, width), bf16),
         "up": V((2, samples, width), bf16),
         "v": V((rank, width), bf16),
         "u": V((rank, width), bf16),
-        "pg": V((2 * samples, width), bf16),
+        "pg": V((2, samples, width), bf16),
         "hid": V((2 * samples, rank), bf16),
         "hgr": V((2 * samples, rank), bf16),
-        "hid_t": V((rank, 2 * samples), bf16),
-        "hgr_t": V((rank, 2 * samples), bf16),
+        "hid_t": V((2, rank, samples), bf16),
+        "hgr_t": V((2, rank, samples), bf16),
         "ids": V((2, n_tbl, slots_dev, hot, samples), i32),
-        "pt": V((2, TABLES, half, EMB), f32),
         "slot": pltpu.SMEM((TABLES,), i32),
         "inv": pltpu.SMEM((slots_dev * n_tbl,), i32),
         "load_sem": pltpu.SemaphoreType.DMA((4,)),
-        "in_s": pltpu.SemaphoreType.DMA((2,)),
-        "in_r": pltpu.SemaphoreType.DMA((2,)),
+        "in_s": pltpu.SemaphoreType.DMA((10,)),
+        "in_r": pltpu.SemaphoreType.DMA((10,)),
         "id_s": pltpu.SemaphoreType.DMA((2, n_tbl)),
         "id_r": pltpu.SemaphoreType.DMA((2, n_tbl)),
-        "ssem": pltpu.SemaphoreType.DMA((16,)),
-        "rsem": pltpu.SemaphoreType.DMA((16,)),
+        "ssem": pltpu.SemaphoreType.DMA((20,)),
+        "rsem": pltpu.SemaphoreType.DMA((20,)),
     }
     lead = ((2, 2, 2), (2, 2), (2,), ())
-    for name, first, tile in (
-        ("a", (2, 2, 2), (16, cut)),
-        ("b", (2, 2, 2), (16, rest)),
-        ("c", None, tab),
-        ("d", (2, 2, 2), tab),
+    for name, tile in (
+        ("a", (16, cuts[1] - cuts[0])),
+        ("b", (16, cuts[2] - cuts[1])),
+        ("e", (16, cuts[3] - cuts[2])),
+        ("c", tab),
+        ("d", tab),
     ):
         for k in range(4):
             shape = lead[k] + tile
-            if name == "c" and k == 0:
+            if name in "cd" and k == 0:
                 shape = (TABLES, half, EMB)
             out["s%s%d" % (name, k)] = V(shape, bf16)
             out["r%s%d" % (name, k)] = V(shape, bf16)
@@ -109,7 +109,7 @@
     return out
 
 
-def fused_body(n_grp, n_tbl, scale, cut, names, *refs):
+def fused_body(n_grp, n_tbl, scale, cuts, names, *refs):
     f32, bf16 = jnp.float32, jnp.bfloat16
     ci_hbm, up_hbm, v_hbm, u_hbm, bias_ref, place_ref, ids_hbm, cross_ref, table_ref = refs[:9]
     r = dict(zip(names, refs[9:]))
@@ -162,6 +162,20 @@
             which = jnp.where(targets[i] == q, i, which)
         r["inv"][q] = which
 
+    nt = (((1,), (1,)), ((), ()))
+    own_rows, their_rows = pl.ds(0, samples), pl.ds(samples, samples)
+    loads[0].wait()
+    loads[1].wait()
+    hidden = lax.dot_general(r["ci"][0], r["v"][...], nt, preferred_element_type=f32)
+    r["hid"][own_rows, :] = hidden.astype(bf16)
+    r["hid_t"][0] = hidden.T.astype(bf16)
+    loads[2].wait()
+    loads[3].wait()
+    r["pg"][0] = (r["up"][0].astype(f32) * r["ci"][0].astype(f32)).astype(bf16)
+    hgrad = lax.dot_general(r["pg"][0], r["u"][...], nt, preferred_element_type=f32)
+    r["hgr"][own_rows, :] = hgrad.astype(bf16)
+    r["hgr_t"][0] = hgrad.T.astype(bf16)
+
     pl.semaphore_wait(barrier, 2 * n_tbl)
 
     def remote(src, dst, s, rs, gg, tt):
@@ -172,9 +186,16 @@
         copy.start()
         return copy
 
+    pieces = [pl.ds(cuts[i], cuts[i + 1] - cuts[i]) for i in range(3)]
+    moves = [(r["hid_t"].at[0], r["hid_t"].at[1]), (r["hgr_t"].at[0], r["hgr_t"].at[1])]
+    for cols in pieces:
+        moves.append((ci_hbm.at[:, cols], r["ci"].at[1, :, cols]))
+        moves.append((up_hbm.at[:, cols], r["up"].at[1, :, cols]))
+    moves.append((r["hid"].at[own_rows], r["hid"].at[their_rows]))
+    moves.append((r["hgr"].at[own_rows], r["hgr"].at[their_rows]))
     in_copies = [
-        remote(ci_hbm, r["ci"].at[1], r["in_s"].at[0], r["in_r"].at[0], og, t),
-        remote(up_hbm, r["up"].at[1], r["in_s"].at[1], r["in_r"].at[1], og, t),
+        remote(src, dst, r["in_s"].at[i], r["in_r"].at[i], og, t)
+        for i, (src, dst) in enumerate(moves)
     ]
     id_copies = []
     for step in range(n_tbl):
@@ -191,58 +212,42 @@
             remote(block, r["ids"].at[1, t], r["id_s"].at[1, step], r["id_r"].at[1, step], og, to)
         )
 
-    nt = (((1,), (1,)), ((), ()))
-
-    def forward(who):
-        row = who * samples
-        rows = pl.ds(row, samples)
-        if who == 0:
-            loads[0].wait()
-            loads[1].wait()
-        else:
-            in_copies[0].wait()
-        hidden = lax.dot_general(r["ci"][who], r["v"][...], nt, preferred_element_type=f32)
-        r["hid"][rows, :] = hidden.astype(bf16)
-        r["hid_t"][:, rows] = hidden.T.astype(bf16)
-        if who == 0:
-            loads[2].wait()
-            loads[3].wait()
-        else:
-            in_copies[1].wait()
-        r["pg"][rows, :] = (r["up"][who].astype(f32) * r["ci"][who].astype(f32)).astype(bf16)
-        hgrad = lax.dot_general(r["pg"][rows, :], r["u"][...], nt, preferred_element_type=f32)
-        r["hgr"][rows, :] = hgrad.astype(bf16)
-        r["hgr_t"][:, rows] = hgrad.T.astype(bf16)
-
-    forward(0)
-    forward(1)
-
     quarter = rank // n_grp
 
     def picked(ref):
-        mine_rows = ref[pl.ds(pl.multiple_of((core + 2 * x) * quarter, quarter), quarter), :]
-        other_rows = ref[pl.ds(pl.multiple_of((core + 2 - 2 * x) * quarter, quarter), quarter), :]
-        return jnp.concatenate([mine_rows, other_rows], axis=0)
-
+        both = []
+        for who in range(2):
+            for start in (core + 2 * x, core + 2 - 2 * x):
+                at = pl.ds(pl.multiple_of(start * quarter, quarter), quarter)
+                both.append(ref[who, at, :])
+        return [jnp.concatenate(both[:2], axis=0), jnp.concatenate(both[2:], axis=0)]
+
+    in_copies[0].wait()
+    in_copies[1].wait()
     hsel, gsel = picked(r["hid_t"]), picked(r["hgr_t"])
 
     def blocks(lo, hi):
-        left = jnp.dot(hsel, r["pg"][:, lo:hi], preferred_element_type=f32)
-        right = jnp.dot(gsel[:, :samples], r["ci"][0, :, lo:hi], preferred_element_type=f32)
-        right += jnp.dot(gsel[:, samples:], r["ci"][1, :, lo:hi], preferred_element_type=f32)
+        theirs = r["ci"][1, :, lo:hi]
+        product = (r["up"][1, :, lo:hi].astype(f32) * theirs.astype(f32)).astype(bf16)
+        left = jnp.dot(hsel[0], r["pg"][0, :, lo:hi], preferred_element_type=f32)
+        left += jnp.dot(hsel[1], product, preferred_element_type=f32)
+        right = jnp.dot(gsel[0], r["ci"][0, :, lo:hi], preferred_element_type=f32)
+        right += jnp.dot(gsel[1], theirs, preferred_element_type=f32)
         return [
             jnp.concatenate([left[8 * d : 8 * d + 8], right[8 * d : 8 * d + 8]], axis=0)
             for d in range(2 * n_tbl)
         ]
 
-    for lo in range(0, cut, 512):
-        hi = min(lo + 512, cut)
+    in_copies[2].wait()
+    in_copies[3].wait()
+    for lo in range(cuts[0], cuts[1], 512):
+        hi = min(lo + 512, cuts[1])
         made = blocks(lo, hi)
         for d in range(n_tbl):
             at = (d // 4, (d // 2) % 2, d % 2, slice(None), slice(lo, hi))
             r["oa0"][at] = made[d]
             r["sa0"][at] = made[n_tbl + d].astype(bf16)
-    sems = iter(range(16))
+    sems = iter(range(20))
 
     def send(name, k, gg, tt):
         i = next(sems)
@@ -251,17 +256,33 @@
         )
 
     a0 = send("a", 0, xg, t)
-    for lo in range(cut, width, 512):
-        hi = min(lo + 512, width)
+    in_copies[4].wait()
+    in_copies[5].wait()
+    for lo in range(cuts[1], cuts[2], 512):
+        hi = min(lo + 512, cuts[2])
         made = blocks(lo, hi)
         for side in range(2):
             xx = x if side == 0 else 1 - x
             for z in range(n_tbl // 2):
                 even, odd = made[side * n_tbl + 2 * z], made[side * n_tbl + 2 * z + 1]
-                at = (xx, z // 2, z % 2, slice(None), slice(lo - cut, hi - cut))
+                at = (xx, z // 2, z % 2, slice(None), slice(lo - cuts[1], hi - cuts[1]))
                 r["ob0"][at] = jnp.where(y == 0, even, odd)
                 r["sb0"][at] = jnp.where(y == 0, odd, even).astype(bf16)
     b0 = send("b", 0, g, yt)
+    in_copies[6].wait()
+    in_copies[7].wait()
+    for lo in range(cuts[2], cuts[3], 512):
+        hi = min(lo + 512, cuts[3])
+        made = blocks(lo, hi)
+        for side in range(2):
+            xx = x if side == 0 else 1 - x
+            for z in range(2):
+                for yy in range(2):
+                    first = side * n_tbl + 4 * z + yy
+                    at = (xx, z, yy, slice(None), slice(lo - cuts[2], hi - cuts[2]))
+                    r["oe0"][at] = jnp.where(zl == 0, made[first], made[first + 2])
+                    r["se0"][at] = jnp.where(zl == 0, made[first + 2], made[first]).astype(bf16)
+    e0 = send("e", 0, g, zlt)
 
     def indices(depth):
         out = [()]
@@ -320,18 +341,18 @@
                 )
             r["oc0"][table] = sums[:half]
             r["sc0"][table] = sums[part : part + half].astype(bf16)
-            r["pt"][x, table] = sums[half:part]
-            r["pt"][1 - x, table] = sums[part + half :]
+            r["od0"][table] = sums[half:part]
+            r["sd0"][table] = sums[part + half :].astype(bf16)
         return carry
 
+    in_copies[8].wait()
+    in_copies[9].wait()
     mine.wait()
     for copy in id_copies:
         copy.wait()
-    early = TABLES // 4
-    lax.fori_loop(0, early, tables, 0)
-    a1 = halve("a", 0, 2, y, g, yt, a0)
-    lax.fori_loop(early, TABLES // 2, tables, 0)
+    lax.fori_loop(0, TABLES // 2, tables, 0)
     c0 = send("c", 0, xg, t)
+    d0 = send("d", 0, xg, t)
 
     def each_slot(yy, put):
         def run(i, carry):
@@ -344,34 +365,33 @@
 
         lax.fori_loop(0, slots_dev * n_tbl // 2, run, 0)
 
-    def put_d(ref, kind):
-        def put(at, which, there):
-            for xx in range(2):
-                ref[(xx, *at)] = (r["pt"][xx, which] * there).astype(kind)
-
-        return put
-
-    def put_c(ref, kind):
-        def put(at, which, there):
-            ref[at] = ((r["oc0"][which] + r["rc0"][which].astype(f32)) * there).astype(kind)
-
-        return put
-
-    each_slot(1 - y, put_d(r["sd0"], bf16))
-    d0 = send("d", 0, g, yt)
+    def put(name, dst, kind):
+        def store(at, which, there):
+            value = r["o%s0" % name][which] + r["r%s0" % name][which].astype(f32)
+            dst[at] = (value * there).astype(kind)
+
+        return store
+
+    def spread(name, before):
+        before.wait()
+        each_slot(1 - y, put(name, r["s%s1" % name], bf16))
+        copy = send(name, 1, g, yt)
+        each_slot(y, put(name, r["o%s1" % name], f32))
+        return copy
+
+    a1 = halve("a", 0, 2, y, g, yt, a0)
+    e1 = halve("e", 0, 1, zh, g, zht, e0)
     b1 = halve("b", 0, 0, x, xg, t, b0)
-    each_slot(y, put_d(r["od0"], f32))
+    c1 = spread("c", c0)
     a2 = halve("a", 1, 1, zl, g, zlt, a1)
-    c0.wait()
-    each_slot(1 - y, put_c(r["sc1"], bf16))
-    c1 = send("c", 1, g, yt)
-    each_slot(y, put_c(r["oc1"], f32))
-    d1 = halve("d", 0, 0, x, xg, t, d0)
+    e2 = halve("e", 1, 0, x, xg, t, e1)
+    d1 = spread("d", d0)
+    b2 = halve("b", 1, 1, zl, g, zlt, b1)
     a3 = halve("a", 2, 0, zh, g, zht, a2)
-    b2 = halve("b", 1, 1, zl, g, zlt, b1)
     c2 = halve("c", 1, 1, zl, g, zlt, c1)
+    e3 = halve("e", 2, 0, y, g, yt, e2)
+    b3 = halve("b", 2, 0, zh, g, zht, b2)
     d2 = halve("d", 1, 1, zl, g, zlt, d1)
-    b3 = halve("b", 2, 0, zh, g, zht, b2)
     c3 = halve("c", 2, 0, zh, g, zht, c2)
     d3 = halve("d", 2, 0, zh, g, zht, d2)
 
@@ -383,10 +403,9 @@
         cross_ref[:, lo:hi] = value[:8]
         cross_ref[:, width + lo : width + hi] = value[8:]
 
-    a3.wait()
-    finish(total("a"), 0, cut)
-    b3.wait()
-    finish(total("b"), cut, width)
+    for name, copy, i in (("a", a3, 0), ("b", b3, 1), ("e", e3, 2)):
+        copy.wait()
+        finish(total(name), cuts[i], cuts[i + 1])
     c3.wait()
     table_ref[:, :half, :] = total("c")
     d3.wait()
@@ -406,8 +425,9 @@
     slots_dev, hot = owned_ids.shape[:2]
     scale = 1.0 / math.sqrt(samples * n_grp * n_tbl)
     part = ROWS // n_grp
-    cut = (width // EMB // 2) * EMB
-    scratch = scratch_of(samples, width, rank, n_tbl, slots_dev, hot, part, cut)
+    tiles = width // EMB
+    cuts = (0, tiles * 7 // 27 * EMB, tiles * 18 // 27 * EMB, width)
+    scratch = scratch_of(samples, width, rank, n_tbl, slots_dev, hot, part, cuts)
     vmem = pl.BlockSpec(memory_space=pltpu.VMEM)
     smem = pl.BlockSpec(memory_space=pltpu.SMEM)
     hbm = pl.BlockSpec(memory_space=pl.ANY)
@@ -416,7 +436,7 @@
         jax.ShapeDtypeStruct((slots_dev, part, EMB), jnp.float32),
     )
     sums = pl.pallas_call(
-        functools.partial(fused_body, n_grp, n_tbl, scale, cut, tuple(scratch)),
+        functools.partial(fused_body, n_grp, n_tbl, scale, cuts, tuple(scratch)),
         out_shape=shapes,
         in_specs=[hbm] * 4 + [vmem, smem, hbm],
         out_specs=(vmem, vmem),

time: 54.5 us -> 53.3 us (0.978)
  Pallas kernels: 53.6 us -> 52.4 us
    pallas_call x1, Pallas kernels: 51.8 us -> 50.6 us  [on_device_fused(): pl.pallas_call(functools.partial(fused_body, n_grp, n_tbl, scale, cuts, t...]
where the time goes in v3:
time: 53.3 us; the launch traced here: 53.1 us
  Pallas kernels  52.4 us (98%)
  between operations  0.64 us (1%)
    pallas_call x1, Pallas kernels, on_device_fused(): pl.pallas_call(functools.partial(fused_body, n_grp, n_tbl, scale, cuts, t...  50.6 us
    pallas_call x1, Pallas kernels, on_device_fused(): pl.pallas_call(copy_body, out_shape=shapes, in_specs=[vmem, vmem], out_sp...  1.78 us

profile of v3, /device:TPU:0, one launch (start us, length us, event | category | flops | bytes accessed | tf_op | source)
XLA Modules:
  0.0 53.1 jit_solution(4564576310564746159)
XLA Ops:
  0.6 50.6 %cross_backward.1 = (f32[8,6912]{1,0:T(8,128)}, f32[5,64,128]{2,1,0:T(8,128)}) custom-call(bf16[128,3456]{1,0:T(8,128)(2,1)} %refs_0_.1, bf16[128,3456]{1,0:T(8,128)(2,1)} %refs_1_.1, bf16[256,3456]{1,0:T(8,128)(2,1)} %refs_2_.1, bf16[256,3456]{1,0:T(8,128)(2,1)} %refs_3_.1, f32[27,128]{1,0:T(8,128)} %bitcast.1, s32[26]{0:T(128)} %refs_5_.1, ...), custom_call_target="tpu_custom_call" | custom-call | tf_op jit(solution)/shard_map/cross_backward/pallas_call | solution.py:438
  51.3 1.8 %hand_over.1 = (f32[8,6912]{1,0:T(8,128)}, f32[5,64,128]{2,1,0:T(8,128)}) custom-call(f32[8,6912]{1,0:T(8,128)} %get-tuple-element.4.cross_ref, f32[5,64,128]{2,1,0:T(8,128)} %get-tuple-element.5.table_ref), custom_call_target="tpu_custom_call" | custom-call | tf_op jit(solution)/shard_map/hand_over/pallas_call | solution.py:452

commit v4 on v3

--- a/solution.py
+++ b/solution.py
@@ -386,13 +386,13 @@
     a2 = halve("a", 1, 1, zl, g, zlt, a1)
     e2 = halve("e", 1, 0, x, xg, t, e1)
     d1 = spread("d", d0)
-    b2 = halve("b", 1, 1, zl, g, zlt, b1)
     a3 = halve("a", 2, 0, zh, g, zht, a2)
     c2 = halve("c", 1, 1, zl, g, zlt, c1)
+    b2 = halve("b", 1, 1, zl, g, zlt, b1)
     e3 = halve("e", 2, 0, y, g, yt, e2)
-    b3 = halve("b", 2, 0, zh, g, zht, b2)
     d2 = halve("d", 1, 1, zl, g, zlt, d1)
     c3 = halve("c", 2, 0, zh, g, zht, c2)
+    b3 = halve("b", 2, 0, zh, g, zht, b2)
     d3 = halve("d", 2, 0, zh, g, zht, d2)
 
     def total(name):

time: 53.3 us -> 50.6 us (0.949)
  Pallas kernels: 52.4 us -> 49.7 us
    pallas_call x1, Pallas kernels: 50.6 us -> 47.9 us  [on_device_fused(): pl.pallas_call(functools.partial(fused_body, n_grp, n_tbl, scale, cuts, t...]
where the time goes in v4:
time: 50.6 us; the launch traced here: 50.3 us
  Pallas kernels  49.7 us (98%)
  between operations  0.64 us (1%)
    pallas_call x1, Pallas kernels, on_device_fused(): pl.pallas_call(functools.partial(fused_body, n_grp, n_tbl, scale, cuts, t...  47.9 us
    pallas_call x1, Pallas kernels, on_device_fused(): pl.pallas_call(copy_body, out_shape=shapes, in_specs=[vmem, vmem], out_sp...  1.78 us

profile of v4, /device:TPU:0, one launch (start us, length us, event | category | flops | bytes accessed | tf_op | source)
XLA Modules:
  0.0 50.3 jit_solution(14411809881777867022)
XLA Ops:
  0.6 47.9 %cross_backward.1 = (f32[8,6912]{1,0:T(8,128)}, f32[5,64,128]{2,1,0:T(8,128)}) custom-call(bf16[128,3456]{1,0:T(8,128)(2,1)} %refs_0_.1, bf16[128,3456]{1,0:T(8,128)(2,1)} %refs_1_.1, bf16[256,3456]{1,0:T(8,128)(2,1)} %refs_2_.1, bf16[256,3456]{1,0:T(8,128)(2,1)} %refs_3_.1, f32[27,128]{1,0:T(8,128)} %bitcast.1, s32[26]{0:T(128)} %refs_5_.1, ...), custom_call_target="tpu_custom_call" | custom-call | tf_op jit(solution)/shard_map/cross_backward/pallas_call | solution.py:438
  48.6 1.8 %hand_over.1 = (f32[8,6912]{1,0:T(8,128)}, f32[5,64,128]{2,1,0:T(8,128)}) custom-call(f32[8,6912]{1,0:T(8,128)} %get-tuple-element.4.cross_ref, f32[5,64,128]{2,1,0:T(8,128)} %get-tuple-element.5.table_ref), custom_call_target="tpu_custom_call" | custom-call | tf_op jit(solution)/shard_map/hand_over/pallas_call | solution.py:452
